TPU v7x, 256 devices: a whole 4x4x8 slice. The times are simulated.
256 devices in a mesh: seq: 16 (over z, core), rep: 16 (over x, y).
Axes of the slice: x: 4, y: 4, z: 8, core: 2. Of those that a mesh axis runs over, the one named last changes fastest.
Arguments:
- tokens: bfloat16 [65536, 1024], P(('rep', 'seq')), parts along dimension 0, may hold values from -16 to 16
- segments: int32 [65536], P(('rep', 'seq')), parts along dimension 0, may hold values from 0 to 3, never falling along the last dimension, each value on 1 to 2048 neighbouring positions
- qkv_weight: bfloat16 [1024, 3072], replicated, may hold values from -1 to 1
- out_weight: bfloat16 [1024, 1024], replicated, may hold values from -0.1875 to 0.1875
- out_bias: float32 [1024], replicated, may hold values from -3 to 3
- ln_gain: float32 [1024], replicated, may hold values from 0.1 to 1.9
- ln_bias: float32 [1024], replicated, may hold values from -3 to 3
Outputs:
- normed: bfloat16 [65536, 1024], P(('rep', 'seq')), parts along dimension 0
- kv_cache: bfloat16 [65536, 2048], P('rep', 'seq'), parts along dimension 0
There are 16 independent parts, one for each index of `rep`. A program takes and returns all parts, laid end to end along the dimension named above; an argument that names none is the same for every part. Nothing has to cross between parts.
Inputs may be any that keep to these rules, and one draw needn't show every extreme that they name: `segments`: each prompt is a contiguous run of 1 to 2048 tokens, numbers never falling, one prompt exactly 2048 tokens.
All inputs are finite; a program needn't handle non-finite values.
Results may differ from a plain program's by a relative error of at most 0.008.
Values may be sent and summed in bfloat16 or wider, within the bound.
A program may use at most 128 MiB of HBM per device.

v0:
```python
import math
import jax
import jax.numpy as jnp
from jax import lax
from jax.sharding import PartitionSpec as P

HEADS = 16
HEAD = 64
Q_CHUNK = 512


def shards(tokens, segments, qkv_weight, out_weight, out_bias, ln_gain, ln_bias):
    tok_rows, width = tokens.shape
    scale = 1.0 / math.sqrt(HEAD)
    all_seg = lax.all_gather(segments, "seq", axis=0, tiled=True)
    proj = jnp.dot(tokens, qkv_weight, preferred_element_type=jnp.float32).astype(jnp.bfloat16)
    grouped = proj.reshape(tok_rows, HEADS, 3 * HEAD)
    mine = lax.all_to_all(grouped, "seq", split_axis=1, concat_axis=0, tiled=True)
    count_rows = mine.shape[0]
    mine = mine.reshape(count_rows, 3 * HEAD)
    kv_cache = mine[:, HEAD:]
    query = mine[:, :HEAD]
    key_h = mine[:, HEAD : 2 * HEAD]
    value_h = mine[:, 2 * HEAD :]
    chunks = count_rows // Q_CHUNK

    def per_chunk(items):
        q_c, seg_c = items
        kept = seg_c[:, None] == all_seg[None, :]
        score = jnp.dot(q_c, key_h.T, preferred_element_type=jnp.float32) * scale
        score = jnp.where(kept, score, -1e30)
        top = jnp.max(score, axis=1, keepdims=True)
        weight = jnp.where(kept, jnp.exp(score - top), 0.0)
        total = jnp.sum(weight, axis=1, keepdims=True)
        acc = jnp.dot(weight.astype(jnp.bfloat16), value_h, preferred_element_type=jnp.float32)
        return (acc / total).astype(jnp.bfloat16)

    context = lax.map(
        per_chunk, (query.reshape(chunks, Q_CHUNK, HEAD), all_seg.reshape(chunks, Q_CHUNK))
    ).reshape(count_rows, 1, HEAD)
    gathered_ctx = lax.all_to_all(context, "seq", split_axis=0, concat_axis=1, tiled=True)
    gathered_ctx = gathered_ctx.reshape(tok_rows, width)
    mixed = (
        jnp.dot(gathered_ctx, out_weight, preferred_element_type=jnp.float32)
        + out_bias
        + tokens.astype(jnp.float32)
    )
    mean = jnp.mean(mixed, axis=1, keepdims=True)
    centered = mixed - mean
    variance = jnp.mean(centered * centered, axis=1, keepdims=True)
    normed = centered / jnp.sqrt(variance + 1e-05) * ln_gain + ln_bias
    return (normed.astype(jnp.bfloat16), kv_cache)


def solution(mesh):
    in_specs = (P(("rep", "seq"), None), P(("rep", "seq")), P(), P(), P(), P(), P())
    out_specs = (P(("rep", "seq"), None), P("rep", "seq"))
    return jax.shard_map(shards, mesh=mesh, in_specs=in_specs, out_specs=out_specs, check_vma=False)
```

profile of v0, /device:TPU:1, one launch (start us, length us, event | category | flops | bytes accessed | tf_op | source)
XLA Modules:
  0.0 213.7 jit_solution(3142455166517597984)
XLA Ops:
  0.7 6.0 %convolution_convert_fusion = bf16[256,3072]{1,0:T(8,128)(2,1)} fusion(bf16[256,1024]{1,0:T(8,128)(2,1)} %param.9, bf16[1024,3072]{1,0:T(8,128)(2,1)} %param.11), kind=kOutput, calls=%fused_computation.18 | convolution fusion | flops 1611399168 | bytes 8388608 | tf_op jit(solution)/shard_map/dot_general | solution.py:16
  9.3 10.0 %all-to-all-start = ((bf16[256,16,192]{0,2,1:T(8,128)(2,1)}), bf16[256,16,192]{0,2,1:T(8,128)(2,1)}, u32[]{:S(2)}, u32[]{:S(2)}) async-start(bf16[256,16,192]{0,2,1:T(8,128)(2,1)} %bitcast.51), calls=%async_computation | async-start | bytes 3145728 | tf_op jit(solution)/shard_map/all_to_all | solution.py:18
  19.3 48.2 %all-gather = s32[16,1,256]{2,1,0:T(1,128)S(1)} all-gather(s32[1,1,256]{2,1,0:T(1,128)S(1)} %bitcast.60), channel_id=1, replica_groups=mesh['seq'=16,'rep'=16] {'seq'}, dimensions={0}, use_global_device_ids=true | all-gather | bytes 17408 | tf_op jit(solution)/shard_map/all_gather | solution.py:15
  76.2 70.4 %while.10 = (s32[]{:T(128)}, bf16[8,512,64]{1,2,0:T(8,128)(2,1)}, s32[8,512]{1,0:T(8,128)S(1)}, s32[4096]{0:T(1024)S(1)}, bf16[8,512,64]{2,1,0:T(8,128)(2,1)}, /...) while((s32[]{:T(128)}, bf16[8,512,64]{1,2,0:T(8,128)(2,1)}, s32[8,512]{1,0:T(8,128)S(1)}, ...), condition=%wide.region_3.4_spmd, body=%wide.region_0.3_spmd.sunk | while | flops 570489856 | bytes 29102212 | solution.py:38
  76.3 2.9 %fusion.42 = (f32[512]{0:T(512)S(1)}, f32[512,4096]{1,0:T(8,128)S(1)}) fusion(s32[4096]{0:T(1024)S(1)} %get-tuple-element.145, s32[512]{0:T(512)S(1)} %bitcast.57, bf16[4096,64]{1,0:T(8,128)(2,1)} %get-tuple-element.147, bf16[8,512,64]{2,1,0:T(8,128)(2,1)} %get-tuple-element.146, s32[]{:T(128)S(6)} %copy.40), kind=kOutput, calls=%fused_computation.2.clone.1 | convolution fusion | flops 276823552 | bytes 9588740 | tf_op jit(solution)/shard_map/while/body/eval_jaxpr/dot_general | solution.py:30
  79.1 2.6 %fusion.43 = f32[512]{0:T(512)S(1)} fusion(f32[512,4096]{1,0:T(8,128)S(1)} %get-tuple-element.124, f32[512]{0:T(512)S(1)} %get-tuple-element.125, s32[4096]{0:T(1024)S(1)} %get-tuple-element.145, s32[512]{0:T(512)S(1)} %bitcast.58), kind=kLoop, calls=%fused_computation.3.clone.1 | loop fusion | flops 12582400 | bytes 8411136 | tf_op jit(solution)/shard_map/while/body/eval_jaxpr/reduce_sum | solution.py:34
  81.8 3.3 %fusion.44 = bf16[8,512,64]{1,2,0:T(8,128)(2,1)} fusion(bf16[8,512,64]{1,2,0:T(8,128)(2,1)} %get-tuple-element.135, s32[]{:T(128)S(6)} %copy.40, bf16[4096,64]{1,0:T(8,128)(2,1)S(1)} %copy-done.2, f32[512,4096]{1,0:T(8,128)S(1)} %get-tuple-element.124, f32[512]{0:T(512)S(1)} %get-tuple-element.125, s32[4096]{0:T(1024)S(1)} %get-tuple-element.145, ...), kind=kOutput, calls=%fused_computation.9.clone.1 | convolution fusion | flops 281083904 | bytes 9000964 | tf_op jit(solution)/shard_map/while/body/eval_jaxpr/dot_general | solution.py:35
  85.1 2.9 %fusion.42 = (f32[512]{0:T(512)S(1)}, f32[512,4096]{1,0:T(8,128)S(1)}) fusion(s32[4096]{0:T(1024)S(1)} %get-tuple-element.145, s32[512]{0:T(512)S(1)} %bitcast.57, bf16[4096,64]{1,0:T(8,128)(2,1)} %get-tuple-element.147, bf16[8,512,64]{2,1,0:T(8,128)(2,1)} %get-tuple-element.146, s32[]{:T(128)S(6)} %copy.40), kind=kOutput, calls=%fused_computation.2.clone.1 | convolution fusion | flops 276823552 | bytes 9588740 | tf_op jit(solution)/shard_map/while/body/eval_jaxpr/dot_general | solution.py:30
  87.9 2.6 %fusion.43 = f32[512]{0:T(512)S(1)} fusion(f32[512,4096]{1,0:T(8,128)S(1)} %get-tuple-element.124, f32[512]{0:T(512)S(1)} %get-tuple-element.125, s32[4096]{0:T(1024)S(1)} %get-tuple-element.145, s32[512]{0:T(512)S(1)} %bitcast.58), kind=kLoop, calls=%fused_computation.3.clone.1 | loop fusion | flops 12582400 | bytes 8411136 | tf_op jit(solution)/shard_map/while/body/eval_jaxpr/reduce_sum | solution.py:34
  90.6 3.3 %fusion.44 = bf16[8,512,64]{1,2,0:T(8,128)(2,1)} fusion(bf16[8,512,64]{1,2,0:T(8,128)(2,1)} %get-tuple-element.135, s32[]{:T(128)S(6)} %copy.40, bf16[4096,64]{1,0:T(8,128)(2,1)S(1)} %copy-done.2, f32[512,4096]{1,0:T(8,128)S(1)} %get-tuple-element.124, f32[512]{0:T(512)S(1)} %get-tuple-element.125, s32[4096]{0:T(1024)S(1)} %get-tuple-element.145, ...), kind=kOutput, calls=%fused_computation.9.clone.1 | convolution fusion | flops 281083904 | bytes 9000964 | tf_op jit(solution)/shard_map/while/body/eval_jaxpr/dot_general | solution.py:35
  93.9 2.9 %fusion.42 = (f32[512]{0:T(512)S(1)}, f32[512,4096]{1,0:T(8,128)S(1)}) fusion(s32[4096]{0:T(1024)S(1)} %get-tuple-element.145, s32[512]{0:T(512)S(1)} %bitcast.57, bf16[4096,64]{1,0:T(8,128)(2,1)} %get-tuple-element.147, bf16[8,512,64]{2,1,0:T(8,128)(2,1)} %get-tuple-element.146, s32[]{:T(128)S(6)} %copy.40), kind=kOutput, calls=%fused_computation.2.clone.1 | convolution fusion | flops 276823552 | bytes 9588740 | tf_op jit(solution)/shard_map/while/body/eval_jaxpr/dot_general | solution.py:30
  96.7 2.6 %fusion.43 = f32[512]{0:T(512)S(1)} fusion(f32[512,4096]{1,0:T(8,128)S(1)} %get-tuple-element.124, f32[512]{0:T(512)S(1)} %get-tuple-element.125, s32[4096]{0:T(1024)S(1)} %get-tuple-element.145, s32[512]{0:T(512)S(1)} %bitcast.58), kind=kLoop, calls=%fused_computation.3.clone.1 | loop fusion | flops 12582400 | bytes 8411136 | tf_op jit(solution)/shard_map/while/body/eval_jaxpr/reduce_sum | solution.py:34
  99.4 3.3 %fusion.44 = bf16[8,512,64]{1,2,0:T(8,128)(2,1)} fusion(bf16[8,512,64]{1,2,0:T(8,128)(2,1)} %get-tuple-element.135, s32[]{:T(128)S(6)} %copy.40, bf16[4096,64]{1,0:T(8,128)(2,1)S(1)} %copy-done.2, f32[512,4096]{1,0:T(8,128)S(1)} %get-tuple-element.124, f32[512]{0:T(512)S(1)} %get-tuple-element.125, s32[4096]{0:T(1024)S(1)} %get-tuple-element.145, ...), kind=kOutput, calls=%fused_computation.9.clone.1 | convolution fusion | flops 281083904 | bytes 9000964 | tf_op jit(solution)/shard_map/while/body/eval_jaxpr/dot_general | solution.py:35
  102.7 2.9 %fusion.42 = (f32[512]{0:T(512)S(1)}, f32[512,4096]{1,0:T(8,128)S(1)}) fusion(s32[4096]{0:T(1024)S(1)} %get-tuple-element.145, s32[512]{0:T(512)S(1)} %bitcast.57, bf16[4096,64]{1,0:T(8,128)(2,1)} %get-tuple-element.147, bf16[8,512,64]{2,1,0:T(8,128)(2,1)} %get-tuple-element.146, s32[]{:T(128)S(6)} %copy.40), kind=kOutput, calls=%fused_computation.2.clone.1 | convolution fusion | flops 276823552 | bytes 9588740 | tf_op jit(solution)/shard_map/while/body/eval_jaxpr/dot_general | solution.py:30
  105.5 2.6 %fusion.43 = f32[512]{0:T(512)S(1)} fusion(f32[512,4096]{1,0:T(8,128)S(1)} %get-tuple-element.124, f32[512]{0:T(512)S(1)} %get-tuple-element.125, s32[4096]{0:T(1024)S(1)} %get-tuple-element.145, s32[512]{0:T(512)S(1)} %bitcast.58), kind=kLoop, calls=%fused_computation.3.clone.1 | loop fusion | flops 12582400 | bytes 8411136 | tf_op jit(solution)/shard_map/while/body/eval_jaxpr/reduce_sum | solution.py:34
  108.2 3.3 %fusion.44 = bf16[8,512,64]{1,2,0:T(8,128)(2,1)} fusion(bf16[8,512,64]{1,2,0:T(8,128)(2,1)} %get-tuple-element.135, s32[]{:T(128)S(6)} %copy.40, bf16[4096,64]{1,0:T(8,128)(2,1)S(1)} %copy-done.2, f32[512,4096]{1,0:T(8,128)S(1)} %get-tuple-element.124, f32[512]{0:T(512)S(1)} %get-tuple-element.125, s32[4096]{0:T(1024)S(1)} %get-tuple-element.145, ...), kind=kOutput, calls=%fused_computation.9.clone.1 | convolution fusion | flops 281083904 | bytes 9000964 | tf_op jit(solution)/shard_map/while/body/eval_jaxpr/dot_general | solution.py:35
  111.5 2.9 %fusion.42 = (f32[512]{0:T(512)S(1)}, f32[512,4096]{1,0:T(8,128)S(1)}) fusion(s32[4096]{0:T(1024)S(1)} %get-tuple-element.145, s32[512]{0:T(512)S(1)} %bitcast.57, bf16[4096,64]{1,0:T(8,128)(2,1)} %get-tuple-element.147, bf16[8,512,64]{2,1,0:T(8,128)(2,1)} %get-tuple-element.146, s32[]{:T(128)S(6)} %copy.40), kind=kOutput, calls=%fused_computation.2.clone.1 | convolution fusion | flops 276823552 | bytes 9588740 | tf_op jit(solution)/shard_map/while/body/eval_jaxpr/dot_general | solution.py:30
  114.3 2.6 %fusion.43 = f32[512]{0:T(512)S(1)} fusion(f32[512,4096]{1,0:T(8,128)S(1)} %get-tuple-element.124, f32[512]{0:T(512)S(1)} %get-tuple-element.125, s32[4096]{0:T(1024)S(1)} %get-tuple-element.145, s32[512]{0:T(512)S(1)} %bitcast.58), kind=kLoop, calls=%fused_computation.3.clone.1 | loop fusion | flops 12582400 | bytes 8411136 | tf_op jit(solution)/shard_map/while/body/eval_jaxpr/reduce_sum | solution.py:34
  117.0 3.3 %fusion.44 = bf16[8,512,64]{1,2,0:T(8,128)(2,1)} fusion(bf16[8,512,64]{1,2,0:T(8,128)(2,1)} %get-tuple-element.135, s32[]{:T(128)S(6)} %copy.40, bf16[4096,64]{1,0:T(8,128)(2,1)S(1)} %copy-done.2, f32[512,4096]{1,0:T(8,128)S(1)} %get-tuple-element.124, f32[512]{0:T(512)S(1)} %get-tuple-element.125, s32[4096]{0:T(1024)S(1)} %get-tuple-element.145, ...), kind=kOutput, calls=%fused_computation.9.clone.1 | convolution fusion | flops 281083904 | bytes 9000964 | tf_op jit(solution)/shard_map/while/body/eval_jaxpr/dot_general | solution.py:35
  120.3 2.9 %fusion.42 = (f32[512]{0:T(512)S(1)}, f32[512,4096]{1,0:T(8,128)S(1)}) fusion(s32[4096]{0:T(1024)S(1)} %get-tuple-element.145, s32[512]{0:T(512)S(1)} %bitcast.57, bf16[4096,64]{1,0:T(8,128)(2,1)} %get-tuple-element.147, bf16[8,512,64]{2,1,0:T(8,128)(2,1)} %get-tuple-element.146, s32[]{:T(128)S(6)} %copy.40), kind=kOutput, calls=%fused_computation.2.clone.1 | convolution fusion | flops 276823552 | bytes 9588740 | tf_op jit(solution)/shard_map/while/body/eval_jaxpr/dot_general | solution.py:30
  123.1 2.6 %fusion.43 = f32[512]{0:T(512)S(1)} fusion(f32[512,4096]{1,0:T(8,128)S(1)} %get-tuple-element.124, f32[512]{0:T(512)S(1)} %get-tuple-element.125, s32[4096]{0:T(1024)S(1)} %get-tuple-element.145, s32[512]{0:T(512)S(1)} %bitcast.58), kind=kLoop, calls=%fused_computation.3.clone.1 | loop fusion | flops 12582400 | bytes 8411136 | tf_op jit(solution)/shard_map/while/body/eval_jaxpr/reduce_sum | solution.py:34
  125.8 3.3 %fusion.44 = bf16[8,512,64]{1,2,0:T(8,128)(2,1)} fusion(bf16[8,512,64]{1,2,0:T(8,128)(2,1)} %get-tuple-element.135, s32[]{:T(128)S(6)} %copy.40, bf16[4096,64]{1,0:T(8,128)(2,1)S(1)} %copy-done.2, f32[512,4096]{1,0:T(8,128)S(1)} %get-tuple-element.124, f32[512]{0:T(512)S(1)} %get-tuple-element.125, s32[4096]{0:T(1024)S(1)} %get-tuple-element.145, ...), kind=kOutput, calls=%fused_computation.9.clone.1 | convolution fusion | flops 281083904 | bytes 9000964 | tf_op jit(solution)/shard_map/while/body/eval_jaxpr/dot_general | solution.py:35
  129.1 2.9 %fusion.42 = (f32[512]{0:T(512)S(1)}, f32[512,4096]{1,0:T(8,128)S(1)}) fusion(s32[4096]{0:T(1024)S(1)} %get-tuple-element.145, s32[512]{0:T(512)S(1)} %bitcast.57, bf16[4096,64]{1,0:T(8,128)(2,1)} %get-tuple-element.147, bf16[8,512,64]{2,1,0:T(8,128)(2,1)} %get-tuple-element.146, s32[]{:T(128)S(6)} %copy.40), kind=kOutput, calls=%fused_computation.2.clone.1 | convolution fusion | flops 276823552 | bytes 9588740 | tf_op jit(solution)/shard_map/while/body/eval_jaxpr/dot_general | solution.py:30
  134.6 3.3 %fusion.44 = bf16[8,512,64]{1,2,0:T(8,128)(2,1)} fusion(bf16[8,512,64]{1,2,0:T(8,128)(2,1)} %get-tuple-element.135, s32[]{:T(128)S(6)} %copy.40, bf16[4096,64]{1,0:T(8,128)(2,1)S(1)} %copy-done.2, f32[512,4096]{1,0:T(8,128)S(1)} %get-tuple-element.124, f32[512]{0:T(512)S(1)} %get-tuple-element.125, s32[4096]{0:T(1024)S(1)} %get-tuple-element.145, ...), kind=kOutput, calls=%fused_computation.9.clone.1 | convolution fusion | flops 281083904 | bytes 9000964 | tf_op jit(solution)/shard_map/while/body/eval_jaxpr/dot_general | solution.py:35
  137.9 2.9 %fusion.42 = (f32[512]{0:T(512)S(1)}, f32[512,4096]{1,0:T(8,128)S(1)}) fusion(s32[4096]{0:T(1024)S(1)} %get-tuple-element.145, s32[512]{0:T(512)S(1)} %bitcast.57, bf16[4096,64]{1,0:T(8,128)(2,1)} %get-tuple-element.147, bf16[8,512,64]{2,1,0:T(8,128)(2,1)} %get-tuple-element.146, s32[]{:T(128)S(6)} %copy.40), kind=kOutput, calls=%fused_computation.2.clone.1 | convolution fusion | flops 276823552 | bytes 9588740 | tf_op jit(solution)/shard_map/while/body/eval_jaxpr/dot_general | solution.py:30
  143.4 3.3 %fusion.44 = bf16[8,512,64]{1,2,0:T(8,128)(2,1)} fusion(bf16[8,512,64]{1,2,0:T(8,128)(2,1)} %get-tuple-element.135, s32[]{:T(128)S(6)} %copy.40, bf16[4096,64]{1,0:T(8,128)(2,1)S(1)} %copy-done.2, f32[512,4096]{1,0:T(8,128)S(1)} %get-tuple-element.124, f32[512]{0:T(512)S(1)} %get-tuple-element.125, s32[4096]{0:T(1024)S(1)} %get-tuple-element.145, ...), kind=kOutput, calls=%fused_computation.9.clone.1 | convolution fusion | flops 281083904 | bytes 9000964 | tf_op jit(solution)/shard_map/while/body/eval_jaxpr/dot_general | solution.py:35
  148.2 3.2 %reshape.53 = bf16[4096,1,64]{2,1,0:T(2,128)(2,1)} reshape(bf16[8,512,64]{2,1,0:T(8,128)(2,1)S(1)} %copy.32) | data formatting | bytes 1048576 | tf_op jit(solution)/shard_map/reshape | solution.py:40
  151.9 23.5 %reduce.1 = bf16[4096,64]{1,0:T(8,128)(2,1)S(1)} reduce(bf16[4096,1,64]{2,1,0:T(2,128)(2,1)} %reshape.53, bf16[]{:T(256)} %broadcast.45), dimensions={1}, to_apply=%reshape.53.reduce_sub_computation | reduce | bytes 1048578 | tf_op jit(solution)/shard_map/reshape | solution.py:40
  176.8 5.9 %all-to-all-start.1 = ((bf16[16,2,8192]{2,1,0:T(2,128)(2,1)}), bf16[16,2,8192]{2,1,0:T(2,128)(2,1)}, u32[]{:S(2)}, u32[]{:S(2)}) async-start(bf16[16,2,8192]{2,1,0:T(2,128)(2,1)} %reshape.55), calls=%async_computation.1 | async-start | bytes 1048576 | tf_op jit(solution)/shard_map/all_to_all | solution.py:41
  185.4 14.7 %all-to-all-done.1 = bf16[16,2,8192]{2,1,0:T(2,128)(2,1)} async-done(((bf16[16,2,8192]{2,1,0:T(2,128)(2,1)}), bf16[16,2,8192]{2,1,0:T(2,128)(2,1)}, u32[]{:S(2)}, u32[]{:S(2)}) %all-to-all-start.1) | async-done | bytes 524320 | tf_op jit(solution)/shard_map/all_to_all | solution.py:41
  200.1 5.5 %reshape.56 = bf16[4096,1,64]{2,1,0:T(2,128)(2,1)} reshape(bf16[16,2,8192]{2,1,0:T(2,128)(2,1)} %all-to-all-done.1) | data formatting | bytes 1048576
  205.6 4.6 %copy.28 = bf16[4096,1,64]{0,2,1:T(8,128)(2,1)S(1)} copy(bf16[4096,1,64]{2,1,0:T(2,128)(2,1)} %reshape.56) | data formatting | bytes 1048576 | tf_op jit(solution)/shard_map/all_to_all | solution.py:41
  (60 shorter events, 26.3 us)
Async XLA Ops:
  0.6 209.9 %copy-start = (bf16[1024,1024]{1,0:T(8,128)(2,1)S(1)}, bf16[1024,1024]{1,0:T(8,128)(2,1)}, u32[]{:S(2)}) copy-start(bf16[1024,1024]{1,0:T(8,128)(2,1)} %param.12) | copy-start | bytes 6291460
  0.6 18.6 %copy-start.6 = (s32[256]{0:T(256)S(1)}, s32[256]{0:T(256)}, u32[]{:S(2)}) copy-start(s32[256]{0:T(256)} %param.10) | copy-start | bytes 3076
  9.3 58.2 %all-to-all-start = ((bf16[256,16,192]{0,2,1:T(8,128)(2,1)}), bf16[256,16,192]{0,2,1:T(8,128)(2,1)}, u32[]{:S(2)}, u32[]{:S(2)}) async-start(bf16[256,16,192]{0,2,1:T(8,128)(2,1)} %bitcast.51), calls=%async_computation | async-start | bytes 3145728 | tf_op jit(solution)/shard_map/all_to_all | solution.py:18
  69.1 1.2 copy-start.1
  76.2 5.5 %copy-start.2 = (bf16[4096,64]{1,0:T(8,128)(2,1)S(1)}, bf16[4096,64]{1,0:T(8,128)(2,1)}, u32[]{:S(2)}) copy-start(bf16[4096,64]{1,0:T(8,128)(2,1)} %get-tuple-element.148) | copy-start | bytes 1572868 | tf_op jit(solution)/shard_map/while
  85.1 5.5 %copy-start.2 = (bf16[4096,64]{1,0:T(8,128)(2,1)S(1)}, bf16[4096,64]{1,0:T(8,128)(2,1)}, u32[]{:S(2)}) copy-start(bf16[4096,64]{1,0:T(8,128)(2,1)} %get-tuple-element.148) | copy-start | bytes 1572868 | tf_op jit(solution)/shard_map/while
  93.9 5.5 %copy-start.2 = (bf16[4096,64]{1,0:T(8,128)(2,1)S(1)}, bf16[4096,64]{1,0:T(8,128)(2,1)}, u32[]{:S(2)}) copy-start(bf16[4096,64]{1,0:T(8,128)(2,1)} %get-tuple-element.148) | copy-start | bytes 1572868 | tf_op jit(solution)/shard_map/while
  102.7 5.5 %copy-start.2 = (bf16[4096,64]{1,0:T(8,128)(2,1)S(1)}, bf16[4096,64]{1,0:T(8,128)(2,1)}, u32[]{:S(2)}) copy-start(bf16[4096,64]{1,0:T(8,128)(2,1)} %get-tuple-element.148) | copy-start | bytes 1572868 | tf_op jit(solution)/shard_map/while
  111.5 5.5 %copy-start.2 = (bf16[4096,64]{1,0:T(8,128)(2,1)S(1)}, bf16[4096,64]{1,0:T(8,128)(2,1)}, u32[]{:S(2)}) copy-start(bf16[4096,64]{1,0:T(8,128)(2,1)} %get-tuple-element.148) | copy-start | bytes 1572868 | tf_op jit(solution)/shard_map/while
  120.3 5.5 %copy-start.2 = (bf16[4096,64]{1,0:T(8,128)(2,1)S(1)}, bf16[4096,64]{1,0:T(8,128)(2,1)}, u32[]{:S(2)}) copy-start(bf16[4096,64]{1,0:T(8,128)(2,1)} %get-tuple-element.148) | copy-start | bytes 1572868 | tf_op jit(solution)/shard_map/while
  129.1 5.5 %copy-start.2 = (bf16[4096,64]{1,0:T(8,128)(2,1)S(1)}, bf16[4096,64]{1,0:T(8,128)(2,1)}, u32[]{:S(2)}) copy-start(bf16[4096,64]{1,0:T(8,128)(2,1)} %get-tuple-element.148) | copy-start | bytes 1572868 | tf_op jit(solution)/shard_map/while
  137.9 5.5 %copy-start.2 = (bf16[4096,64]{1,0:T(8,128)(2,1)S(1)}, bf16[4096,64]{1,0:T(8,128)(2,1)}, u32[]{:S(2)}) copy-start(bf16[4096,64]{1,0:T(8,128)(2,1)} %get-tuple-element.148) | copy-start | bytes 1572868 | tf_op jit(solution)/shard_map/while
  151.9 58.6 %copy-start.3 = (f32[1024]{0:T(1024)S(1)}, f32[1024]{0:T(1024)}, u32[]{:S(2)}) copy-start(f32[1024]{0:T(1024)} %param.13) | copy-start | bytes 12292
  176.8 23.2 %all-to-all-start.1 = ((bf16[16,2,8192]{2,1,0:T(2,128)(2,1)}), bf16[16,2,8192]{2,1,0:T(2,128)(2,1)}, u32[]{:S(2)}, u32[]{:S(2)}) async-start(bf16[16,2,8192]{2,1,0:T(2,128)(2,1)} %reshape.55), calls=%async_computation.1 | async-start | bytes 1048576 | tf_op jit(solution)/shard_map/all_to_all | solution.py:41
  182.8 29.9 %copy-start.4 = (f32[1024]{0:T(1024)S(1)}, f32[1024]{0:T(1024)}, u32[]{:S(2)}) copy-start(f32[1024]{0:T(1024)} %param.15) | copy-start | bytes 12292
  182.8 29.9 %copy-start.5 = (f32[1024]{0:T(1024)S(1)}, f32[1024]{0:T(1024)}, u32[]{:S(2)}) copy-start(f32[1024]{0:T(1024)} %param.14) | copy-start | bytes 12292
where the time goes:
time: 215 us; the launch traced here: 214 us
  matrix products  57.2 us (27%)
  blocking collectives  48.2 us (22%)
  other arithmetic  45.8 us (21%)
  local copies, waits for them, and re-layouts  31.1 us (14%)
  starting transfers between devices  15.9 us (7%)
  waiting for transfers between devices  14.7 us (7%)
    all_gather x1, blocking collectives, shards(): all_seg = lax.all_gather(segments, 'seq', axis=0, tiled=True)  48.2 us
    dot_general x8, matrix products, per_chunk(): jnp.dot(weight.astype(jnp.bfloat16), value_h, preferred_element_type=jnp....  26.4 us
    reshape x1, other arithmetic, shards(): context = lax.map(per_chunk, (query.reshape(chunks, Q_CHUNK, HEAD), all_s...  23.5 us
    dot_general x8, matrix products, per_chunk(): score = jnp.dot(q_c, key_h.T, preferred_element_type=jnp.float32) * scale  22.9 us
    reduce_sum x8, other arithmetic, per_chunk(): total = jnp.sum(weight, axis=1, keepdims=True)  21 us
    all_to_all x1, waiting for transfers between devices, shards(): lax.all_to_all(context, 'seq', split_axis=0, concat_axis=1, tiled=True)  14.7 us
    unnamed x17, local copies, waits for them, and re-layouts  11.2 us
    all_to_all x1, starting transfers between devices, shards(): lax.all_to_all(grouped, 'seq', split_axis=1, concat_axis=0, tiled=True)  9.97 us
  transfers between devices with their start and end apart: 2, of which 1 were waited for; matrix products, arithmetic and copies ran while one was open for 1% of the time, Pallas kernels for 0%

commit v1 on v0

--- a/solution.py
+++ b/solution.py
@@ -9,10 +9,15 @@
 Q_CHUNK = 512
 
 
+def gather_by_exchange(x, axis, dim):
+    copies = jnp.concatenate([x] * lax.axis_size(axis), axis=dim)
+    return lax.all_to_all(copies, axis, dim, dim, tiled=True)
+
+
 def shards(tokens, segments, qkv_weight, out_weight, out_bias, ln_gain, ln_bias):
     tok_rows, width = tokens.shape
     scale = 1.0 / math.sqrt(HEAD)
-    all_seg = lax.all_gather(segments, "seq", axis=0, tiled=True)
+    all_seg = gather_by_exchange(segments, "seq", 0)
     proj = jnp.dot(tokens, qkv_weight, preferred_element_type=jnp.float32).astype(jnp.bfloat16)
     grouped = proj.reshape(tok_rows, HEADS, 3 * HEAD)
     mine = lax.all_to_all(grouped, "seq", split_axis=1, concat_axis=0, tiled=True)

time: 215 us -> 212 us (0.986)
  blocking collectives: 48.2 us -> 0 us
  waiting for transfers between devices: 14.7 us -> 53.2 us
  starting transfers between devices: 15.9 us -> 21.3 us
    all_gather x1 -> x0, blocking collectives: 48.2 us -> none  [shards(): all_seg = lax.all_gather(segments, 'seq', axis=0, tiled=True)]
    all_to_all x1, waiting for transfers between devices: 0.01 us -> 38.6 us  [shards(): lax.all_to_all(grouped, 'seq', split_axis=1, concat_axis=0, tiled=True)]
    all_to_all x0 -> x1, starting transfers between devices: none -> 9.97 us  [gather_by_exchange(): return lax.all_to_all(copies, axis, dim, dim, tiled=True)]
    all_to_all x1, starting transfers between devices: 9.97 us -> 7.23 us  [shards(): lax.all_to_all(grouped, 'seq', split_axis=1, concat_axis=0, tiled=True)]
    unnamed x17 -> x15, local copies, waits for them, and re-layouts: 11.2 us -> 11.2 us
  transfers between devices with their start and end apart: 2 -> 3, of which waited for: 1 -> 2; matrix products, arithmetic and copies ran while one was open for 1% -> 5% of each run, Pallas kernels for 0% -> 0%
where the time goes in v1:
time: 212 us; the launch traced here: 211 us
  matrix products  57.1 us (27%)
  waiting for transfers between devices  53.2 us (25%)
  other arithmetic  45.8 us (22%)
  local copies, waits for them, and re-layouts  32.6 us (15%)
  starting transfers between devices  21.3 us (10%)
    all_to_all x1, waiting for transfers between devices, shards(): lax.all_to_all(grouped, 'seq', split_axis=1, concat_axis=0, tiled=True)  38.6 us
    dot_general x8, matrix products, per_chunk(): jnp.dot(weight.astype(jnp.bfloat16), value_h, preferred_element_type=jnp....  26.4 us
    reshape x1, other arithmetic, shards(): context = lax.map(per_chunk, (query.reshape(chunks, Q_CHUNK, HEAD), all_s...  23.5 us
    dot_general x8, matrix products, per_chunk(): score = jnp.dot(q_c, key_h.T, preferred_element_type=jnp.float32) * scale  22.9 us
    reduce_sum x8, other arithmetic, per_chunk(): total = jnp.sum(weight, axis=1, keepdims=True)  21 us
    all_to_all x1, waiting for transfers between devices, shards(): lax.all_to_all(context, 'seq', split_axis=0, concat_axis=1, tiled=True)  14.7 us
    unnamed x15, local copies, waits for them, and re-layouts  11.2 us
    all_to_all x1, starting transfers between devices, gather_by_exchange(): return lax.all_to_all(copies, axis, dim, dim, tiled=True)  9.97 us
  transfers between devices with their start and end apart: 3, of which 2 were waited for; matrix products, arithmetic and copies ran while one was open for 5% of the time, Pallas kernels for 0%

profile of v1, /device:TPU:1, one launch (start us, length us, event | category | flops | bytes accessed | tf_op | source)
XLA Modules:
  0.0 210.8 jit_solution(17934647127701508251)
XLA Ops:
  2.1 10.0 %all-to-all-start = ((s32[16,256,1]{1,2,0:T(1,128)}), s32[16,256,1]{1,2,0:T(1,128)S(1)}, u32[]{:S(2)}, u32[]{:S(2)}) async-start(s32[16,256,1]{1,2,0:T(1,128)} %concatenate.4), calls=%async_computation | async-start | bytes 32768 | tf_op jit(solution)/shard_map/all_to_all | solution.py:14
  12.1 5.9 %convolution_convert_fusion = bf16[256,3072]{1,0:T(8,128)(2,1)} fusion(bf16[256,1024]{1,0:T(8,128)(2,1)} %param.9, bf16[1024,3072]{1,0:T(8,128)(2,1)} %param.11), kind=kOutput, calls=%fused_computation.18 | convolution fusion | flops 1611399168 | bytes 8388608 | tf_op jit(solution)/shard_map/dot_general | solution.py:21
  20.6 7.2 %all-to-all-start.1 = ((bf16[256,16,192]{0,2,1:T(8,128)(2,1)}), bf16[256,16,192]{0,2,1:T(8,128)(2,1)}, u32[]{:S(2)}, u32[]{:S(2)}) async-start(bf16[256,16,192]{0,2,1:T(8,128)(2,1)} %bitcast.50), calls=%async_computation.1 | async-start | bytes 3145728 | tf_op jit(solution)/shard_map/all_to_all | solution.py:23
  27.9 38.6 %all-to-all-done.1 = bf16[256,16,192]{0,2,1:T(8,128)(2,1)} async-done(((bf16[256,16,192]{0,2,1:T(8,128)(2,1)}), bf16[256,16,192]{0,2,1:T(8,128)(2,1)}, u32[]{:S(2)}, u32[]{:S(2)}) %all-to-all-start.1) | async-done | bytes 1572896 | tf_op jit(solution)/shard_map/all_to_all | solution.py:23
  75.2 70.4 %while.10 = (s32[]{:T(128)}, bf16[8,512,64]{1,2,0:T(8,128)(2,1)}, s32[8,512]{1,0:T(8,128)S(1)}, s32[4096]{0:T(1024)S(1)}, bf16[8,512,64]{2,1,0:T(8,128)(2,1)}, /...) while((s32[]{:T(128)}, bf16[8,512,64]{1,2,0:T(8,128)(2,1)}, s32[8,512]{1,0:T(8,128)S(1)}, ...), condition=%wide.region_3.4_spmd, body=%wide.region_0.3_spmd.sunk | while | flops 570489856 | bytes 29102212 | solution.py:43
  75.2 2.9 %fusion.42 = (f32[512]{0:T(512)S(1)}, f32[512,4096]{1,0:T(8,128)S(1)}) fusion(s32[4096]{0:T(1024)S(1)} %get-tuple-element.145, s32[512]{0:T(512)S(1)} %bitcast.56, bf16[4096,64]{1,0:T(8,128)(2,1)} %get-tuple-element.147, bf16[8,512,64]{2,1,0:T(8,128)(2,1)} %get-tuple-element.146, s32[]{:T(128)S(6)} %copy.40), kind=kOutput, calls=%fused_computation.2.clone.1 | convolution fusion | flops 276823552 | bytes 9588740 | tf_op jit(solution)/shard_map/while/body/eval_jaxpr/dot_general | solution.py:35
  78.0 2.6 %fusion.43 = f32[512]{0:T(512)S(1)} fusion(f32[512,4096]{1,0:T(8,128)S(1)} %get-tuple-element.124, f32[512]{0:T(512)S(1)} %get-tuple-element.125, s32[4096]{0:T(1024)S(1)} %get-tuple-element.145, s32[512]{0:T(512)S(1)} %bitcast.57), kind=kLoop, calls=%fused_computation.3.clone.1 | loop fusion | flops 12582400 | bytes 8411136 | tf_op jit(solution)/shard_map/while/body/eval_jaxpr/reduce_sum | solution.py:39
  80.7 3.3 %fusion.44 = bf16[8,512,64]{1,2,0:T(8,128)(2,1)} fusion(bf16[8,512,64]{1,2,0:T(8,128)(2,1)} %get-tuple-element.135, s32[]{:T(128)S(6)} %copy.40, bf16[4096,64]{1,0:T(8,128)(2,1)S(1)} %copy-done.2, f32[512,4096]{1,0:T(8,128)S(1)} %get-tuple-element.124, f32[512]{0:T(512)S(1)} %get-tuple-element.125, s32[4096]{0:T(1024)S(1)} %get-tuple-element.145, ...), kind=kOutput, calls=%fused_computation.9.clone.1 | convolution fusion | flops 281083904 | bytes 9000964 | tf_op jit(solution)/shard_map/while/body/eval_jaxpr/dot_general | solution.py:40
  84.0 2.9 %fusion.42 = (f32[512]{0:T(512)S(1)}, f32[512,4096]{1,0:T(8,128)S(1)}) fusion(s32[4096]{0:T(1024)S(1)} %get-tuple-element.145, s32[512]{0:T(512)S(1)} %bitcast.56, bf16[4096,64]{1,0:T(8,128)(2,1)} %get-tuple-element.147, bf16[8,512,64]{2,1,0:T(8,128)(2,1)} %get-tuple-element.146, s32[]{:T(128)S(6)} %copy.40), kind=kOutput, calls=%fused_computation.2.clone.1 | convolution fusion | flops 276823552 | bytes 9588740 | tf_op jit(solution)/shard_map/while/body/eval_jaxpr/dot_general | solution.py:35
  86.8 2.6 %fusion.43 = f32[512]{0:T(512)S(1)} fusion(f32[512,4096]{1,0:T(8,128)S(1)} %get-tuple-element.124, f32[512]{0:T(512)S(1)} %get-tuple-element.125, s32[4096]{0:T(1024)S(1)} %get-tuple-element.145, s32[512]{0:T(512)S(1)} %bitcast.57), kind=kLoop, calls=%fused_computation.3.clone.1 | loop fusion | flops 12582400 | bytes 8411136 | tf_op jit(solution)/shard_map/while/body/eval_jaxpr/reduce_sum | solution.py:39
  89.5 3.3 %fusion.44 = bf16[8,512,64]{1,2,0:T(8,128)(2,1)} fusion(bf16[8,512,64]{1,2,0:T(8,128)(2,1)} %get-tuple-element.135, s32[]{:T(128)S(6)} %copy.40, bf16[4096,64]{1,0:T(8,128)(2,1)S(1)} %copy-done.2, f32[512,4096]{1,0:T(8,128)S(1)} %get-tuple-element.124, f32[512]{0:T(512)S(1)} %get-tuple-element.125, s32[4096]{0:T(1024)S(1)} %get-tuple-element.145, ...), kind=kOutput, calls=%fused_computation.9.clone.1 | convolution fusion | flops 281083904 | bytes 9000964 | tf_op jit(solution)/shard_map/while/body/eval_jaxpr/dot_general | solution.py:40
  92.8 2.9 %fusion.42 = (f32[512]{0:T(512)S(1)}, f32[512,4096]{1,0:T(8,128)S(1)}) fusion(s32[4096]{0:T(1024)S(1)} %get-tuple-element.145, s32[512]{0:T(512)S(1)} %bitcast.56, bf16[4096,64]{1,0:T(8,128)(2,1)} %get-tuple-element.147, bf16[8,512,64]{2,1,0:T(8,128)(2,1)} %get-tuple-element.146, s32[]{:T(128)S(6)} %copy.40), kind=kOutput, calls=%fused_computation.2.clone.1 | convolution fusion | flops 276823552 | bytes 9588740 | tf_op jit(solution)/shard_map/while/body/eval_jaxpr/dot_general | solution.py:35
  95.6 2.6 %fusion.43 = f32[512]{0:T(512)S(1)} fusion(f32[512,4096]{1,0:T(8,128)S(1)} %get-tuple-element.124, f32[512]{0:T(512)S(1)} %get-tuple-element.125, s32[4096]{0:T(1024)S(1)} %get-tuple-element.145, s32[512]{0:T(512)S(1)} %bitcast.57), kind=kLoop, calls=%fused_computation.3.clone.1 | loop fusion | flops 12582400 | bytes 8411136 | tf_op jit(solution)/shard_map/while/body/eval_jaxpr/reduce_sum | solution.py:39
  98.3 3.3 %fusion.44 = bf16[8,512,64]{1,2,0:T(8,128)(2,1)} fusion(bf16[8,512,64]{1,2,0:T(8,128)(2,1)} %get-tuple-element.135, s32[]{:T(128)S(6)} %copy.40, bf16[4096,64]{1,0:T(8,128)(2,1)S(1)} %copy-done.2, f32[512,4096]{1,0:T(8,128)S(1)} %get-tuple-element.124, f32[512]{0:T(512)S(1)} %get-tuple-element.125, s32[4096]{0:T(1024)S(1)} %get-tuple-element.145, ...), kind=kOutput, calls=%fused_computation.9.clone.1 | convolution fusion | flops 281083904 | bytes 9000964 | tf_op jit(solution)/shard_map/while/body/eval_jaxpr/dot_general | solution.py:40
  101.6 2.9 %fusion.42 = (f32[512]{0:T(512)S(1)}, f32[512,4096]{1,0:T(8,128)S(1)}) fusion(s32[4096]{0:T(1024)S(1)} %get-tuple-element.145, s32[512]{0:T(512)S(1)} %bitcast.56, bf16[4096,64]{1,0:T(8,128)(2,1)} %get-tuple-element.147, bf16[8,512,64]{2,1,0:T(8,128)(2,1)} %get-tuple-element.146, s32[]{:T(128)S(6)} %copy.40), kind=kOutput, calls=%fused_computation.2.clone.1 | convolution fusion | flops 276823552 | bytes 9588740 | tf_op jit(solution)/shard_map/while/body/eval_jaxpr/dot_general | solution.py:35
  107.1 3.3 %fusion.44 = bf16[8,512,64]{1,2,0:T(8,128)(2,1)} fusion(bf16[8,512,64]{1,2,0:T(8,128)(2,1)} %get-tuple-element.135, s32[]{:T(128)S(6)} %copy.40, bf16[4096,64]{1,0:T(8,128)(2,1)S(1)} %copy-done.2, f32[512,4096]{1,0:T(8,128)S(1)} %get-tuple-element.124, f32[512]{0:T(512)S(1)} %get-tuple-element.125, s32[4096]{0:T(1024)S(1)} %get-tuple-element.145, ...), kind=kOutput, calls=%fused_computation.9.clone.1 | convolution fusion | flops 281083904 | bytes 9000964 | tf_op jit(solution)/shard_map/while/body/eval_jaxpr/dot_general | solution.py:40
  110.4 2.9 %fusion.42 = (f32[512]{0:T(512)S(1)}, f32[512,4096]{1,0:T(8,128)S(1)}) fusion(s32[4096]{0:T(1024)S(1)} %get-tuple-element.145, s32[512]{0:T(512)S(1)} %bitcast.56, bf16[4096,64]{1,0:T(8,128)(2,1)} %get-tuple-element.147, bf16[8,512,64]{2,1,0:T(8,128)(2,1)} %get-tuple-element.146, s32[]{:T(128)S(6)} %copy.40), kind=kOutput, calls=%fused_computation.2.clone.1 | convolution fusion | flops 276823552 | bytes 9588740 | tf_op jit(solution)/shard_map/while/body/eval_jaxpr/dot_general | solution.py:35
  115.9 3.3 %fusion.44 = bf16[8,512,64]{1,2,0:T(8,128)(2,1)} fusion(bf16[8,512,64]{1,2,0:T(8,128)(2,1)} %get-tuple-element.135, s32[]{:T(128)S(6)} %copy.40, bf16[4096,64]{1,0:T(8,128)(2,1)S(1)} %copy-done.2, f32[512,4096]{1,0:T(8,128)S(1)} %get-tuple-element.124, f32[512]{0:T(512)S(1)} %get-tuple-element.125, s32[4096]{0:T(1024)S(1)} %get-tuple-element.145, ...), kind=kOutput, calls=%fused_computation.9.clone.1 | convolution fusion | flops 281083904 | bytes 9000964 | tf_op jit(solution)/shard_map/while/body/eval_jaxpr/dot_general | solution.py:40
  119.2 2.9 %fusion.42 = (f32[512]{0:T(512)S(1)}, f32[512,4096]{1,0:T(8,128)S(1)}) fusion(s32[4096]{0:T(1024)S(1)} %get-tuple-element.145, s32[512]{0:T(512)S(1)} %bitcast.56, bf16[4096,64]{1,0:T(8,128)(2,1)} %get-tuple-element.147, bf16[8,512,64]{2,1,0:T(8,128)(2,1)} %get-tuple-element.146, s32[]{:T(128)S(6)} %copy.40), kind=kOutput, calls=%fused_computation.2.clone.1 | convolution fusion | flops 276823552 | bytes 9588740 | tf_op jit(solution)/shard_map/while/body/eval_jaxpr/dot_general | solution.py:35
  122.1 2.6 %fusion.43 = f32[512]{0:T(512)S(1)} fusion(f32[512,4096]{1,0:T(8,128)S(1)} %get-tuple-element.124, f32[512]{0:T(512)S(1)} %get-tuple-element.125, s32[4096]{0:T(1024)S(1)} %get-tuple-element.145, s32[512]{0:T(512)S(1)} %bitcast.57), kind=kLoop, calls=%fused_computation.3.clone.1 | loop fusion | flops 12582400 | bytes 8411136 | tf_op jit(solution)/shard_map/while/body/eval_jaxpr/reduce_sum | solution.py:39
  124.7 3.3 %fusion.44 = bf16[8,512,64]{1,2,0:T(8,128)(2,1)} fusion(bf16[8,512,64]{1,2,0:T(8,128)(2,1)} %get-tuple-element.135, s32[]{:T(128)S(6)} %copy.40, bf16[4096,64]{1,0:T(8,128)(2,1)S(1)} %copy-done.2, f32[512,4096]{1,0:T(8,128)S(1)} %get-tuple-element.124, f32[512]{0:T(512)S(1)} %get-tuple-element.125, s32[4096]{0:T(1024)S(1)} %get-tuple-element.145, ...), kind=kOutput, calls=%fused_computation.9.clone.1 | convolution fusion | flops 281083904 | bytes 9000964 | tf_op jit(solution)/shard_map/while/body/eval_jaxpr/dot_general | solution.py:40
  128.0 2.9 %fusion.42 = (f32[512]{0:T(512)S(1)}, f32[512,4096]{1,0:T(8,128)S(1)}) fusion(s32[4096]{0:T(1024)S(1)} %get-tuple-element.145, s32[512]{0:T(512)S(1)} %bitcast.56, bf16[4096,64]{1,0:T(8,128)(2,1)} %get-tuple-element.147, bf16[8,512,64]{2,1,0:T(8,128)(2,1)} %get-tuple-element.146, s32[]{:T(128)S(6)} %copy.40), kind=kOutput, calls=%fused_computation.2.clone.1 | convolution fusion | flops 276823552 | bytes 9588740 | tf_op jit(solution)/shard_map/while/body/eval_jaxpr/dot_general | solution.py:35
  133.5 3.3 %fusion.44 = bf16[8,512,64]{1,2,0:T(8,128)(2,1)} fusion(bf16[8,512,64]{1,2,0:T(8,128)(2,1)} %get-tuple-element.135, s32[]{:T(128)S(6)} %copy.40, bf16[4096,64]{1,0:T(8,128)(2,1)S(1)} %copy-done.2, f32[512,4096]{1,0:T(8,128)S(1)} %get-tuple-element.124, f32[512]{0:T(512)S(1)} %get-tuple-element.125, s32[4096]{0:T(1024)S(1)} %get-tuple-element.145, ...), kind=kOutput, calls=%fused_computation.9.clone.1 | convolution fusion | flops 281083904 | bytes 9000964 | tf_op jit(solution)/shard_map/while/body/eval_jaxpr/dot_general | solution.py:40
  136.8 2.9 %fusion.42 = (f32[512]{0:T(512)S(1)}, f32[512,4096]{1,0:T(8,128)S(1)}) fusion(s32[4096]{0:T(1024)S(1)} %get-tuple-element.145, s32[512]{0:T(512)S(1)} %bitcast.56, bf16[4096,64]{1,0:T(8,128)(2,1)} %get-tuple-element.147, bf16[8,512,64]{2,1,0:T(8,128)(2,1)} %get-tuple-element.146, s32[]{:T(128)S(6)} %copy.40), kind=kOutput, calls=%fused_computation.2.clone.1 | convolution fusion | flops 276823552 | bytes 9588740 | tf_op jit(solution)/shard_map/while/body/eval_jaxpr/dot_general | solution.py:35
  139.7 2.6 %fusion.43 = f32[512]{0:T(512)S(1)} fusion(f32[512,4096]{1,0:T(8,128)S(1)} %get-tuple-element.124, f32[512]{0:T(512)S(1)} %get-tuple-element.125, s32[4096]{0:T(1024)S(1)} %get-tuple-element.145, s32[512]{0:T(512)S(1)} %bitcast.57), kind=kLoop, calls=%fused_computation.3.clone.1 | loop fusion | flops 12582400 | bytes 8411136 | tf_op jit(solution)/shard_map/while/body/eval_jaxpr/reduce_sum | solution.py:39
  142.3 3.3 %fusion.44 = bf16[8,512,64]{1,2,0:T(8,128)(2,1)} fusion(bf16[8,512,64]{1,2,0:T(8,128)(2,1)} %get-tuple-element.135, s32[]{:T(128)S(6)} %copy.40, bf16[4096,64]{1,0:T(8,128)(2,1)S(1)} %copy-done.2, f32[512,4096]{1,0:T(8,128)S(1)} %get-tuple-element.124, f32[512]{0:T(512)S(1)} %get-tuple-element.125, s32[4096]{0:T(1024)S(1)} %get-tuple-element.145, ...), kind=kOutput, calls=%fused_computation.9.clone.1 | convolution fusion | flops 281083904 | bytes 9000964 | tf_op jit(solution)/shard_map/while/body/eval_jaxpr/dot_general | solution.py:40
  147.1 3.2 %reshape.71 = bf16[4096,1,64]{2,1,0:T(2,128)(2,1)} reshape(bf16[8,512,64]{2,1,0:T(8,128)(2,1)S(1)} %copy.32) | data formatting | bytes 1048576 | tf_op jit(solution)/shard_map/reshape | solution.py:45
  150.8 23.5 %reduce.1 = bf16[4096,64]{1,0:T(8,128)(2,1)S(1)} reduce(bf16[4096,1,64]{2,1,0:T(2,128)(2,1)} %reshape.71, bf16[]{:T(256)} %broadcast.47), dimensions={1}, to_apply=%reshape.71.reduce_sub_computation | reduce | bytes 1048578 | tf_op jit(solution)/shard_map/reshape | solution.py:45
  175.8 4.1 %all-to-all-start.2 = ((bf16[16,2,8192]{2,1,0:T(2,128)(2,1)}), bf16[16,2,8192]{2,1,0:T(2,128)(2,1)}, u32[]{:S(2)}, u32[]{:S(2)}) async-start(bf16[16,2,8192]{2,1,0:T(2,128)(2,1)} %reshape.73), calls=%async_computation.2 | async-start | bytes 1048576 | tf_op jit(solution)/shard_map/all_to_all | solution.py:46
  182.6 14.7 %all-to-all-done.2 = bf16[16,2,8192]{2,1,0:T(2,128)(2,1)} async-done(((bf16[16,2,8192]{2,1,0:T(2,128)(2,1)}), bf16[16,2,8192]{2,1,0:T(2,128)(2,1)}, u32[]{:S(2)}, u32[]{:S(2)}) %all-to-all-start.2) | async-done | bytes 524320 | tf_op jit(solution)/shard_map/all_to_all | solution.py:46
  197.2 5.5 %reshape.74 = bf16[4096,1,64]{2,1,0:T(2,128)(2,1)} reshape(bf16[16,2,8192]{2,1,0:T(2,128)(2,1)} %all-to-all-done.2) | data formatting | bytes 1048576
  202.8 4.6 %copy.28 = bf16[4096,1,64]{0,2,1:T(8,128)(2,1)S(1)} copy(bf16[4096,1,64]{2,1,0:T(2,128)(2,1)} %reshape.74) | data formatting | bytes 1048576 | tf_op jit(solution)/shard_map/all_to_all | solution.py:46
  (60 shorter events, 30.4 us)
Async XLA Ops:
  0.6 207.0 %copy-start = (bf16[1024,1024]{1,0:T(8,128)(2,1)S(1)}, bf16[1024,1024]{1,0:T(8,128)(2,1)}, u32[]{:S(2)}) copy-start(bf16[1024,1024]{1,0:T(8,128)(2,1)} %param.12) | copy-start | bytes 6291460
  2.1 18.5 %all-to-all-start = ((s32[16,256,1]{1,2,0:T(1,128)}), s32[16,256,1]{1,2,0:T(1,128)S(1)}, u32[]{:S(2)}, u32[]{:S(2)}) async-start(s32[16,256,1]{1,2,0:T(1,128)} %concatenate.4), calls=%async_computation | async-start | bytes 32768 | tf_op jit(solution)/shard_map/all_to_all | solution.py:14
  20.6 45.9 %all-to-all-start.1 = ((bf16[256,16,192]{0,2,1:T(8,128)(2,1)}), bf16[256,16,192]{0,2,1:T(8,128)(2,1)}, u32[]{:S(2)}, u32[]{:S(2)}) async-start(bf16[256,16,192]{0,2,1:T(8,128)(2,1)} %bitcast.50), calls=%async_computation.1 | async-start | bytes 3145728 | tf_op jit(solution)/shard_map/all_to_all | solution.py:23
  68.0 1.2 copy-start.1
  75.2 5.5 %copy-start.2 = (bf16[4096,64]{1,0:T(8,128)(2,1)S(1)}, bf16[4096,64]{1,0:T(8,128)(2,1)}, u32[]{:S(2)}) copy-start(bf16[4096,64]{1,0:T(8,128)(2,1)} %get-tuple-element.148) | copy-start | bytes 1572868 | tf_op jit(solution)/shard_map/while
  84.0 5.5 %copy-start.2 = (bf16[4096,64]{1,0:T(8,128)(2,1)S(1)}, bf16[4096,64]{1,0:T(8,128)(2,1)}, u32[]{:S(2)}) copy-start(bf16[4096,64]{1,0:T(8,128)(2,1)} %get-tuple-element.148) | copy-start | bytes 1572868 | tf_op jit(solution)/shard_map/while
  92.8 5.5 %copy-start.2 = (bf16[4096,64]{1,0:T(8,128)(2,1)S(1)}, bf16[4096,64]{1,0:T(8,128)(2,1)}, u32[]{:S(2)}) copy-start(bf16[4096,64]{1,0:T(8,128)(2,1)} %get-tuple-element.148) | copy-start | bytes 1572868 | tf_op jit(solution)/shard_map/while
  101.6 5.5 %copy-start.2 = (bf16[4096,64]{1,0:T(8,128)(2,1)S(1)}, bf16[4096,64]{1,0:T(8,128)(2,1)}, u32[]{:S(2)}) copy-start(bf16[4096,64]{1,0:T(8,128)(2,1)} %get-tuple-element.148) | copy-start | bytes 1572868 | tf_op jit(solution)/shard_map/while
  110.4 5.5 %copy-start.2 = (bf16[4096,64]{1,0:T(8,128)(2,1)S(1)}, bf16[4096,64]{1,0:T(8,128)(2,1)}, u32[]{:S(2)}) copy-start(bf16[4096,64]{1,0:T(8,128)(2,1)} %get-tuple-element.148) | copy-start | bytes 1572868 | tf_op jit(solution)/shard_map/while
  119.2 5.5 %copy-start.2 = (bf16[4096,64]{1,0:T(8,128)(2,1)S(1)}, bf16[4096,64]{1,0:T(8,128)(2,1)}, u32[]{:S(2)}) copy-start(bf16[4096,64]{1,0:T(8,128)(2,1)} %get-tuple-element.148) | copy-start | bytes 1572868 | tf_op jit(solution)/shard_map/while
  128.0 5.5 %copy-start.2 = (bf16[4096,64]{1,0:T(8,128)(2,1)S(1)}, bf16[4096,64]{1,0:T(8,128)(2,1)}, u32[]{:S(2)}) copy-start(bf16[4096,64]{1,0:T(8,128)(2,1)} %get-tuple-element.148) | copy-start | bytes 1572868 | tf_op jit(solution)/shard_map/while
  136.8 5.5 %copy-start.2 = (bf16[4096,64]{1,0:T(8,128)(2,1)S(1)}, bf16[4096,64]{1,0:T(8,128)(2,1)}, u32[]{:S(2)}) copy-start(bf16[4096,64]{1,0:T(8,128)(2,1)} %get-tuple-element.148) | copy-start | bytes 1572868 | tf_op jit(solution)/shard_map/while
  150.8 56.9 %copy-start.3 = (f32[1024]{0:T(1024)S(1)}, f32[1024]{0:T(1024)}, u32[]{:S(2)}) copy-start(f32[1024]{0:T(1024)} %param.13) | copy-start | bytes 12292
  175.8 21.4 %all-to-all-start.2 = ((bf16[16,2,8192]{2,1,0:T(2,128)(2,1)}), bf16[16,2,8192]{2,1,0:T(2,128)(2,1)}, u32[]{:S(2)}, u32[]{:S(2)}) async-start(bf16[16,2,8192]{2,1,0:T(2,128)(2,1)} %reshape.73), calls=%async_computation.2 | async-start | bytes 1048576 | tf_op jit(solution)/shard_map/all_to_all | solution.py:46
  179.9 29.9 %copy-start.4 = (f32[1024]{0:T(1024)S(1)}, f32[1024]{0:T(1024)}, u32[]{:S(2)}) copy-start(f32[1024]{0:T(1024)} %param.15) | copy-start | bytes 12292
  179.9 29.9 %copy-start.5 = (f32[1024]{0:T(1024)S(1)}, f32[1024]{0:T(1024)}, u32[]{:S(2)}) copy-start(f32[1024]{0:T(1024)} %param.14) | copy-start | bytes 12292
